TPU v7x, 512 devices: a whole 4x4x16 slice. The times are simulated.
512 devices in a mesh: dp: 32 (over z, core), fsdp: 16 (over x, y).
Axes of the slice: x: 4, y: 4, z: 16, core: 2. Of those that a mesh axis runs over, the one named last changes fastest.
Arguments:
- gradients: bfloat16 [1, 8192, 28672], P(None, 'fsdp', 'dp'), may hold values from -16 to 16
- errors: bfloat16 [1, 8192, 28672], P(None, 'fsdp', 'dp'), may hold values from -4 to 4
- start_factor: float32 [1, 32, 28672], P(None, None, 'dp'), may hold values from -6 to 6
Outputs:
- compressed: bfloat16 [1, 8192, 28672], P(None, 'fsdp', 'dp')
- new_errors: bfloat16 [1, 8192, 28672], P(None, 'fsdp', 'dp')
All inputs are finite; a program needn't handle non-finite values.
Results may differ from a plain program's by a relative error of at most 0.0085.
Values sent between devices are 32-bit elements; how exact they have to be, the bound alone decides.
No kernel may reach another device: no remote copies, remote signals or barrier semaphores. Data moves between devices by JAX's collectives and lax.ppermute only.
A program may use at most 64 MiB of HBM per device.

v0:
```python
import jax
import jax.numpy as jnp
from jax import lax
from jax.sharding import PartitionSpec as P


def orthonormal(lower, columns):

    def solve_single(factor, right_side):
        return jax.scipy.linalg.solve_triangular(factor, right_side, lower=True)

    return jax.vmap(solve_single)(lower, columns)


def shards(gradients, errors, start_factor):
    combined = (gradients.astype(jnp.float32) + errors.astype(jnp.float32)).astype(jnp.bfloat16)
    factor_low = start_factor.astype(jnp.bfloat16)
    products = jnp.einsum("mrc,mdc->mrd", factor_low, combined, preferred_element_type=jnp.float32)
    summed = lax.psum(products, "dp")
    whole = lax.all_gather(summed, "fsdp", axis=2, tiled=True)
    gram = jnp.einsum(
        "mrd,msd->mrs",
        whole,
        whole,
        precision=lax.Precision.HIGHEST,
        preferred_element_type=jnp.float32,
    )
    lower = jnp.linalg.cholesky(gram)
    basis = orthonormal(lower, summed)
    basis_low = basis.astype(jnp.bfloat16)
    projected = jnp.einsum("mrd,mdc->mrc", basis_low, combined, preferred_element_type=jnp.float32)
    factor_new = lax.psum(projected, "fsdp")
    rebuilt = jnp.einsum(
        "mrd,mrc->mdc",
        basis,
        factor_new,
        precision=lax.Precision.HIGHEST,
        preferred_element_type=jnp.float32,
    )
    compressed = rebuilt.astype(jnp.bfloat16)
    new_errors = (combined.astype(jnp.float32) - rebuilt).astype(jnp.bfloat16)
    return (compressed, new_errors)


def solution(mesh):
    placed = (P(None, "fsdp", "dp"), P(None, "fsdp", "dp"), P(None, None, "dp"))
    return jax.shard_map(
        shards,
        mesh=mesh,
        in_specs=placed,
        out_specs=(P(None, "fsdp", "dp"), P(None, "fsdp", "dp")),
        check_vma=False,
    )
```

profile of v0, /device:TPU:32, one launch (start us, length us, event | category | flops | bytes accessed | tf_op | source)
XLA Modules:
  0.0 389.8 jit_solution(7160317326725971944)
XLA Ops:
  7.2 0.0 all-reduce.3.cloned.1.call-start
  7.2 0.0 copy-start.1
  7.2 2.5 convolution_bitcast_fusion
  9.8 0.0 copy-start
  9.8 0.0 all-reduce.3.cloned.1.call-update
  9.8 0.0 all-gather.2.cloned.1.call-start
  9.8 190.7 %all-reduce.3.cloned.1.call-done = f32[1,32,512]{2,1,0:T(8,128)} async-done(((f32[1,32,512]{2,1,0:T(8,128)}), f32[1,32,512]{2,1,0:T(8,128)}) %all-reduce.3.cloned.1.call-update) | async-done | bytes 65552 | tf_op jit(solution)/shard_map/psum | solution.py:19
  200.5 0.0 all-gather.2.cloned.1.call-update
  200.5 0.0 all-reduce.5.cloned.1.call-start
  200.6 54.9 %all-gather.2.cloned.1.call-done = f32[1,32,8192]{2,1,0:T(8,128)} async-done(((f32[1,32,512]{2,1,0:T(8,128)}), f32[1,32,8192]{2,1,0:T(8,128)}) %all-gather.2.cloned.1.call-update) | async-done | bytes 1048592 | tf_op jit(solution)/shard_map/all_gather | solution.py:20
  255.5 2.5 fusion.1
  258.0 0.1 copy.6
  258.1 2.9 custom-call.8
  261.1 0.6 compare_reduce_fusion
  261.7 0.7 fusion.11
  262.4 2.4 custom-call.9
  264.8 0.0 copy-done.2
  264.8 0.3 fusion.6
  265.1 0.0 copy-done.1
  265.1 0.0 copy-done
  265.1 1.0 fusion.3
  266.1 0.0 all-reduce.5.cloned.1.call-update
  266.1 113.3 %all-reduce.5.cloned.1.call-done = f32[32,896]{1,0:T(8,128)} async-done(((f32[32,896]{1,0:T(8,128)}), f32[32,896]{1,0:T(8,128)}) %all-reduce.5.cloned.1.call-update) | async-done | bytes 114704 | tf_op jit(solution)/shard_map/psum | solution.py:32
  379.4 3.9 fusion
  (3 shorter events, 0.0 us)
Async XLA Ops:
  7.2 193.3 %all-reduce.3.cloned.1.call-start = ((), (), s32[]{:S(2)}) async-start(), calls=%async_computation | async-start | bytes 131072 | tf_op jit(solution)/shard_map/psum | solution.py:19
  7.2 257.9 %copy-start.1 = (bf16[1,512,896]{2,1,0:T(8,128)(2,1)S(1)}, bf16[1,512,896]{2,1,0:T(8,128)(2,1)}, u32[]{:S(2)}) copy-start(bf16[1,512,896]{2,1,0:T(8,128)(2,1)} %param.3) | copy-start | bytes 2752516
  9.8 255.3 %copy-start = (bf16[1,512,896]{2,1,0:T(8,128)(2,1)S(1)}, bf16[1,512,896]{2,1,0:T(8,128)(2,1)}, u32[]{:S(2)}) copy-start(bf16[1,512,896]{2,1,0:T(8,128)(2,1)} %param.4) | copy-start | bytes 2752516
  9.8 245.7 %all-gather.2.cloned.1.call-start = ((), (), s32[]{:S(2)}) async-start(), calls=%async_computation.1 | async-start | bytes 1114112 | tf_op jit(solution)/shard_map/all_gather | solution.py:20
  200.5 64.3 %copy-start.2 = (f32[1,32,512]{2,1,0:T(8,128)S(1)}, f32[1,32,512]{2,1,0:T(8,128)}, u32[]{:S(2)}) copy-start(f32[1,32,512]{2,1,0:T(8,128)} %all-reduce.3.cloned.1.call-done) | copy-start | bytes 196612
  200.5 178.9 %all-reduce.5.cloned.1.call-start = ((), (), s32[]{:S(2)}) async-start(), calls=%async_computation.2 | async-start | bytes 229376 | tf_op jit(solution)/shard_map/psum | solution.py:32
Sparse Core Ops, SparseCore 0:
  10.9 189.5 all-reduce.2
  203.6 51.8 all-gather.1
  266.2 113.1 all-reduce.4
where the time goes:
time: 390 us
  waiting for transfers between devices  359 us (92%)
  between operations  13.8 us (4%)
  matrix products  10.2 us (3%)
  other arithmetic  6.69 us (2%)
    psum x1, waiting for transfers between devices, shards(): summed = lax.psum(products, 'dp')  191 us
    psum x1, waiting for transfers between devices, shards(): factor_new = lax.psum(projected, 'fsdp')  113 us
    all_gather x1, waiting for transfers between devices, shards(): whole = lax.all_gather(summed, 'fsdp', axis=2, tiled=True)  54.9 us
  transfers between devices with their start and end apart: 3, of which 3 were waited for; matrix products, arithmetic and copies ran while one was open for 0% of the time, Pallas kernels for 0%

commit v1 on v0

v1 whole, which is shorter than its diff:
```python
import functools

import jax
import jax.numpy as jnp
from jax import lax
from jax.experimental import pallas as pl
from jax.experimental.pallas import tpu as pltpu
from jax.sharding import PartitionSpec as P

F32 = jnp.float32
BF16 = jnp.bfloat16
RANK = 32
VMEM = pltpu.VMEM


def split3(x):
    a = x.astype(BF16)
    r = x - a.astype(F32)
    b = r.astype(BF16)
    c = (r - b.astype(F32)).astype(BF16)
    return a, b, c


def first_kernel(g_ref, e_ref, s_ref, c_ref, part_ref):
    c = (g_ref[...].astype(F32) + e_ref[...].astype(F32)).astype(BF16)
    c_ref[...] = c
    q = s_ref[...].astype(BF16)
    part_ref[0] = lax.dot_general(q, c, (((1,), (1,)), ((), ())), preferred_element_type=F32)


def first(g, e, s, parts):
    rows, cols = g.shape
    step = rows // parts
    return pl.pallas_call(
        first_kernel,
        grid=(parts,),
        in_specs=[
            pl.BlockSpec((step, cols), lambda i: (i, 0)),
            pl.BlockSpec((step, cols), lambda i: (i, 0)),
            pl.BlockSpec((RANK, cols), lambda i: (0, 0)),
        ],
        out_specs=[
            pl.BlockSpec((step, cols), lambda i: (i, 0)),
            pl.BlockSpec((1, RANK, step), lambda i: (i, 0, 0)),
        ],
        out_shape=[
            jax.ShapeDtypeStruct((rows, cols), BF16),
            jax.ShapeDtypeStruct((parts, RANK, step), F32),
        ],
        compiler_params=pltpu.CompilerParams(vmem_limit_bytes=16 << 20),
        name="first",
    )(g, e, s)


def sum_kernel(copies, x_ref, o_ref):
    total = x_ref[0]
    for k in range(1, x_ref.shape[0]):
        total = total + x_ref[k]
    for k in range(copies):
        o_ref[k] = total


def sum_copies(x, copies):
    return pl.pallas_call(
        functools.partial(sum_kernel, copies),
        out_shape=jax.ShapeDtypeStruct((copies,) + x.shape[1:], F32),
        compiler_params=pltpu.CompilerParams(vmem_limit_bytes=16 << 20),
        name="sum_copies",
    )(x)


def product_kernel(copies, p_ref, c_ref, o_ref):
    parts = p_ref.shape[0]
    terms = [split3(p_ref[k]) for k in range(parts)]
    left = jnp.concatenate([jnp.concatenate([t[j] for t in terms], axis=1) for j in range(3)], axis=0)
    t3 = jnp.dot(left, c_ref[...], preferred_element_type=F32)
    t = t3[:RANK] + t3[RANK : 2 * RANK] + t3[2 * RANK :]
    g3 = lax.dot_general(left, left, (((1,), (1,)), ((), ())), preferred_element_type=F32)
    gr = g3[:RANK] + g3[RANK : 2 * RANK] + g3[2 * RANK :]
    gram = gr[:, :RANK] + gr[:, RANK : 2 * RANK] + gr[:, 2 * RANK : 3 * RANK]
    packed = jnp.concatenate([gram[8 * k : 8 * k + 8] for k in range(4)], axis=1)
    chunks = c_ref.shape[1] // 128
    for k in range(copies):
        for j in range(chunks):
            o_ref[k, j * RANK : (j + 1) * RANK] = t[:, j * 128 : (j + 1) * 128]
        o_ref[k, chunks * RANK : chunks * RANK + 8] = packed


def product(p, c, copies):
    chunks = c.shape[1] // 128
    return pl.pallas_call(
        functools.partial(product_kernel, copies),
        out_shape=jax.ShapeDtypeStruct((copies, chunks * RANK + 8, 128), F32),
        compiler_params=pltpu.CompilerParams(vmem_limit_bytes=16 << 20),
        name="product",
    )(p, c)


def inverse_factor(gram):
    rows = lax.broadcasted_iota(jnp.int32, (RANK, RANK), 0)
    cols = lax.broadcasted_iota(jnp.int32, (RANK, RANK), 1)
    w = jnp.concatenate([gram, (rows == cols).astype(F32)], axis=1)
    below = lax.broadcasted_iota(jnp.int32, (RANK, 1), 0)
    scale = jnp.zeros((RANK, 1), F32)
    for k in range(RANK):
        row = w[k : k + 1]
        inv = 1.0 / row[:, k : k + 1]
        col = jnp.where(below > k, w[:, k : k + 1], 0.0)
        scale = jnp.where(below == k, inv, scale)
        w = w - col * (row * inv)
    return w[:, RANK:] * jnp.sqrt(scale)


def last_kernel(x_ref, p_ref, c_ref, comp_ref, err_ref):
    parts, _, step = p_ref.shape
    chunks = c_ref.shape[1] // 128
    total = x_ref[0]
    for k in range(1, x_ref.shape[0]):
        total = total + x_ref[k]
    t = jnp.concatenate([total[j * RANK : (j + 1) * RANK] for j in range(chunks)], axis=1)
    packed = total[chunks * RANK :]
    gram = jnp.concatenate([packed[:, RANK * k : RANK * (k + 1)] for k in range(4)], axis=0)
    low = inverse_factor(gram)
    f = jnp.dot(low, t, precision=lax.Precision.HIGHEST, preferred_element_type=F32)
    z = lax.dot_general(low, f, (((0,), (0,)), ((), ())), precision=lax.Precision.HIGHEST, preferred_element_type=F32)
    z1, z2, _ = split3(z)
    right = jnp.concatenate([z1, z2, z1], axis=0)
    for k in range(parts):
        p1, p2, _ = split3(p_ref[k])
        left = jnp.concatenate([p1, p1, p2], axis=0)
        rebuilt = lax.dot_general(left, right, (((0,), (0,)), ((), ())), preferred_element_type=F32)
        at = pl.ds(k * step, step)
        comp_ref[at] = rebuilt.astype(BF16)
        err_ref[at] = (c_ref[at].astype(F32) - rebuilt).astype(BF16)


def last(x, p, c):
    return pl.pallas_call(
        last_kernel,
        out_shape=[jax.ShapeDtypeStruct(c.shape, BF16)] * 2,
        compiler_params=pltpu.CompilerParams(vmem_limit_bytes=24 << 20),
        name="last",
    )(x, p, c)


def groups(size, key):
    table = {}
    for i in range(size):
        table.setdefault(key(i), []).append(i)
    return list(table.values())


def shards(near, far, y_groups, x_groups, gradients, errors, start_factor):
    def exchange(x, axis, members):
        return lax.all_to_all(x, axis, 0, 0, tiled=True, axis_index_groups=members)

    parts = len(near[0])
    c, part = first(gradients[0], errors[0], start_factor[0], parts)
    part = exchange(part, "dp", near)
    piece = sum_copies(part, len(far[0]))
    piece = exchange(piece, "dp", far)
    piece = sum_copies(piece, parts)
    p = exchange(piece, "dp", near)
    t = product(p, c, len(y_groups[0]))
    t = exchange(t, "fsdp", y_groups)
    t = sum_copies(t, len(x_groups[0]))
    t = exchange(t, "fsdp", x_groups)
    compressed, new_errors = last(t, p, c)
    return compressed[None], new_errors[None]


def solution(mesh):
    dp, fsdp = mesh.shape["dp"], mesh.shape["fsdp"]
    body = functools.partial(
        shards,
        groups(dp, lambda i: i // 4),
        groups(dp, lambda i: i % 4),
        groups(fsdp, lambda i: i // 4),
        groups(fsdp, lambda i: i % 4),
    )
    return jax.shard_map(
        body,
        mesh=mesh,
        in_specs=(P(None, "fsdp", "dp"), P(None, "fsdp", "dp"), P(None, None, "dp")),
        out_specs=(P(None, "fsdp", "dp"), P(None, "fsdp", "dp")),
        check_vma=False,
    )
```

time: 390 us -> 77.5 us (0.20)
  the two profiles are of different devices: /device:TPU:32 before, /device:TPU:2 now
where the time goes in v1:
time: 77.5 us; the launch traced here: 77.1 us
  blocking collectives  67 us (86%)
  Pallas kernels  6.2 us (8%)
  local copies, waits for them, and re-layouts  3.25 us (4%)
    all_to_all x5, blocking collectives, exchange(): return lax.all_to_all(x, axis, 0, 0, tiled=True, axis_index_groups=members)  67 us
    pallas_call x1, Pallas kernels, last(): pl.pallas_call(last_kernel, out_shape=[jax.ShapeDtypeStruct(c.shape, BF16...  4.88 us
    unnamed x6, local copies, waits for them, and re-layouts  3.25 us

profile of v1, /device:TPU:2, one launch (start us, length us, event | category | flops | bytes accessed | tf_op | source)
XLA Modules:
  0.0 77.1 jit_solution(16286711402490513258)
XLA Ops:
  0.6 0.0 copy-start
  0.6 1.2 %copy-done = bf16[1,512,896]{2,1,0:T(8,128)(2,1)S(1)} copy-done((bf16[1,512,896]{2,1,0:T(8,128)(2,1)S(1)}, bf16[1,512,896]{2,1,0:T(8,128)(2,1)}, u32[]{:S(2)}) %copy-start) | copy-done | bytes 917528
  1.8 0.0 copy-start.1
  1.8 1.2 %copy-done.1 = bf16[1,512,896]{2,1,0:T(8,128)(2,1)S(1)} copy-done((bf16[1,512,896]{2,1,0:T(8,128)(2,1)S(1)}, bf16[1,512,896]{2,1,0:T(8,128)(2,1)}, u32[]{:S(2)}) %copy-start.1) | copy-done | bytes 917528
  3.0 0.0 copy-start.2
  3.0 0.9 %copy-done.2 = f32[1,32,896]{2,1,0:T(8,128)S(1)} copy-done((f32[1,32,896]{2,1,0:T(8,128)S(1)}, f32[1,32,896]{2,1,0:T(8,128)}, u32[]{:S(2)}) %copy-start.2) | copy-done | bytes 114712
  3.9 0.8 %first.1 = (bf16[512,896]{1,0:T(8,128)(2,1)S(1)}, f32[4,32,128]{2,1,0:T(8,128)S(1)}) custom-call(bf16[512,896]{1,0:T(8,128)(2,1)S(1)} %bitcast.5, bf16[512,896]{1,0:T(8,128)(2,1)S(1)} %bitcast.6, f32[32,896]{1,0:T(8,128)S(1)} %bitcast.7), custom_call_target="tpu_custom_call" | custom-call | tf_op jit(solution)/shard_map/first/pallas_call | solution.py:34
  4.7 7.1 %all_to_all.25.x_ref = f32[4,32,128]{2,1,0:T(8,128)S(1)} all-to-all(f32[4,32,128]{2,1,0:T(8,128)S(1)} %get-tuple-element.6), channel_id=1, replica_groups={{0,16,32,48},{64,80,96,112},{128,144,160,176},{192,208,224,240},{256,27..., dimensions={0} | all-to-all | bytes 131072 | tf_op jit(solution)/shard_map/all_to_all | solution.py:155
  11.8 29.4 %all_to_all.26.x_ref = f32[8,32,128]{2,1,0:T(8,128)S(1)} all-to-all(f32[8,32,128]{2,1,0:T(8,128)S(1)} %sum_copies.3), channel_id=1, replica_groups={{0,64,128,192,256,320,384,448},{16,80,144,208,272,336,400,464},{32,96,1..., dimensions={0} | all-to-all | bytes 262144 | tf_op jit(solution)/shard_map/all_to_all | solution.py:155
  41.2 6.5 %all_to_all.27.p_ref = f32[4,32,128]{2,1,0:T(8,128)S(1)} all-to-all(f32[4,32,128]{2,1,0:T(8,128)S(1)} %sum_copies.4), channel_id=1, replica_groups={{0,16,32,48},{64,80,96,112},{128,144,160,176},{192,208,224,240},{256,27..., dimensions={0} | all-to-all | bytes 131072 | tf_op jit(solution)/shard_map/all_to_all | solution.py:155
  47.7 0.5 product.1
  48.2 13.0 %all_to_all.28.x_ref = f32[4,232,128]{2,1,0:T(8,128)S(1)} all-to-all(f32[4,232,128]{2,1,0:T(8,128)S(1)} %product.1), channel_id=1, replica_groups={{0,1,2,3},{4,5,6,7},{8,9,10,11},{12,13,14,15},{16,17,18,19},{20,21,22,2..., dimensions={0} | all-to-all | bytes 950272 | tf_op jit(solution)/shard_map/all_to_all | solution.py:155
  61.2 11.0 %all_to_all.29.x_ref = f32[4,232,128]{2,1,0:T(8,128)S(1)} all-to-all(f32[4,232,128]{2,1,0:T(8,128)S(1)} %sum_copies.5), channel_id=1, replica_groups={{0,4,8,12},{1,5,9,13},{2,6,10,14},{3,7,11,15},{16,20,24,28},{17,21,25,2..., dimensions={0} | all-to-all | bytes 950272 | tf_op jit(solution)/shard_map/all_to_all | solution.py:155
  72.2 4.9 %last.1 = (bf16[512,896]{1,0:T(8,128)(2,1)}, bf16[512,896]{1,0:T(8,128)(2,1)}) custom-call(f32[4,232,128]{2,1,0:T(8,128)S(1)} %all_to_all.29.x_ref, f32[4,32,128]{2,1,0:T(8,128)S(1)} %all_to_all.27.p_ref, bf16[512,896]{1,0:T(8,128)(2,1)S(1)} %get-tuple-element.7.c_ref), custom_call_target="tpu_custom_call" | custom-call | tf_op jit(solution)/shard_map/last/pallas_call | solution.py:138
  (3 shorter events, 0.1 us)
Async XLA Ops:
  0.6 1.2 %copy-start = (bf16[1,512,896]{2,1,0:T(8,128)(2,1)S(1)}, bf16[1,512,896]{2,1,0:T(8,128)(2,1)}, u32[]{:S(2)}) copy-start(bf16[1,512,896]{2,1,0:T(8,128)(2,1)} %param.3) | copy-start | bytes 2752516
  1.8 1.2 %copy-start.1 = (bf16[1,512,896]{2,1,0:T(8,128)(2,1)S(1)}, bf16[1,512,896]{2,1,0:T(8,128)(2,1)}, u32[]{:S(2)}) copy-start(bf16[1,512,896]{2,1,0:T(8,128)(2,1)} %param.4) | copy-start | bytes 2752516
  3.0 0.9 %copy-start.2 = (f32[1,32,896]{2,1,0:T(8,128)S(1)}, f32[1,32,896]{2,1,0:T(8,128)}, u32[]{:S(2)}) copy-start(f32[1,32,896]{2,1,0:T(8,128)} %param.5) | copy-start | bytes 344068

commit v2 on v1

--- a/solution.py
+++ b/solution.py
@@ -21,11 +21,24 @@
     return a, b, c
 
 
-def first_kernel(g_ref, e_ref, s_ref, c_ref, part_ref):
-    c = (g_ref[...].astype(F32) + e_ref[...].astype(F32)).astype(BF16)
-    c_ref[...] = c
-    q = s_ref[...].astype(BF16)
-    part_ref[0] = lax.dot_general(q, c, (((1,), (1,)), ((), ())), preferred_element_type=F32)
+def first_kernel(g_hbm, e_hbm, s_hbm, c_ref, part_ref, g, e, s, sems):
+    parts, _, step = part_ref.shape
+    copies = [pltpu.make_async_copy(s_hbm, s, sems.at[0])]
+    for k in range(parts):
+        at = pl.ds(k * step, step)
+        copies.append(pltpu.make_async_copy(g_hbm.at[at], g.at[at], sems.at[2 * k + 1]))
+        copies.append(pltpu.make_async_copy(e_hbm.at[at], e.at[at], sems.at[2 * k + 2]))
+    for copy in copies:
+        copy.start()
+    copies[0].wait()
+    q = s[...].astype(BF16)
+    for k in range(parts):
+        copies[2 * k + 1].wait()
+        copies[2 * k + 2].wait()
+        at = pl.ds(k * step, step)
+        c = (g[at].astype(F32) + e[at].astype(F32)).astype(BF16)
+        c_ref[at] = c
+        part_ref[k] = lax.dot_general(q, c, (((1,), (1,)), ((), ())), preferred_element_type=F32)
 
 
 def first(g, e, s, parts):
@@ -33,23 +46,20 @@
     step = rows // parts
     return pl.pallas_call(
         first_kernel,
-        grid=(parts,),
-        in_specs=[
-            pl.BlockSpec((step, cols), lambda i: (i, 0)),
-            pl.BlockSpec((step, cols), lambda i: (i, 0)),
-            pl.BlockSpec((RANK, cols), lambda i: (0, 0)),
-        ],
-        out_specs=[
-            pl.BlockSpec((step, cols), lambda i: (i, 0)),
-            pl.BlockSpec((1, RANK, step), lambda i: (i, 0, 0)),
-        ],
+        in_specs=[pl.BlockSpec(memory_space=pltpu.HBM)] * 3,
         out_shape=[
             jax.ShapeDtypeStruct((rows, cols), BF16),
             jax.ShapeDtypeStruct((parts, RANK, step), F32),
         ],
+        scratch_shapes=[
+            VMEM((rows, cols), BF16),
+            VMEM((rows, cols), BF16),
+            VMEM((RANK, cols), F32),
+            pltpu.SemaphoreType.DMA((2 * parts + 1,)),
+        ],
         compiler_params=pltpu.CompilerParams(vmem_limit_bytes=16 << 20),
         name="first",
-    )(g, e, s)
+    )(*[pltpu.with_memory_space_constraint(x, pltpu.HBM) for x in (g, e, s)])
 
 
 def sum_kernel(copies, x_ref, o_ref):
@@ -96,48 +106,71 @@
     )(p, c)
 
 
-def inverse_factor(gram):
-    rows = lax.broadcasted_iota(jnp.int32, (RANK, RANK), 0)
-    cols = lax.broadcasted_iota(jnp.int32, (RANK, RANK), 1)
-    w = jnp.concatenate([gram, (rows == cols).astype(F32)], axis=1)
-    below = lax.broadcasted_iota(jnp.int32, (RANK, 1), 0)
-    scale = jnp.zeros((RANK, 1), F32)
-    for k in range(RANK):
-        row = w[k : k + 1]
-        inv = 1.0 / row[:, k : k + 1]
-        col = jnp.where(below > k, w[:, k : k + 1], 0.0)
-        scale = jnp.where(below == k, inv, scale)
-        w = w - col * (row * inv)
-    return w[:, RANK:] * jnp.sqrt(scale)
-
-
-def last_kernel(x_ref, p_ref, c_ref, comp_ref, err_ref):
+def inverse_factor(gram, block=8):
+    rows = lax.broadcasted_iota(jnp.int32, (RANK, 128), 0)
+    cols = lax.broadcasted_iota(jnp.int32, (RANK, 128), 1)
+    w = jnp.concatenate([gram, jnp.zeros((RANK, 128 - RANK), F32)], axis=1) + (rows + RANK == cols).astype(F32)
+    pivot = jnp.ones((RANK, 128), F32)
+    for first_col in range(0, RANK, block):
+        wide = [jnp.broadcast_to(w[:, k : k + 1], (RANK, 128)) for k in range(first_col, first_col + block)]
+        for j in range(block):
+            k = first_col + j
+            inv = 1.0 / wide[j][k : k + 1]
+            pivot = jnp.where(rows == k, wide[j], pivot)
+            col = jnp.where(rows > k, wide[j], 0.0) * inv
+            for m in range(j + 1, block):
+                wide[m] = wide[m] - col * wide[m][k : k + 1]
+            w = w - col * w[k : k + 1]
+    return (w / jnp.sqrt(pivot))[:, RANK : 2 * RANK]
+
+
+def left_terms(x, axis):
+    a, b, c = split3(x)
+    return jnp.concatenate([a, a, b, a, b, c], axis=axis)
+
+
+def right_terms(x):
+    a, b, c = split3(x)
+    return jnp.concatenate([a, b, a, c, b, a], axis=0)
+
+
+def last_kernel(x_ref, p_ref, c_ref, comp_hbm, err_hbm, comp, err, sems):
     parts, _, step = p_ref.shape
     chunks = c_ref.shape[1] // 128
     total = x_ref[0]
     for k in range(1, x_ref.shape[0]):
         total = total + x_ref[k]
-    t = jnp.concatenate([total[j * RANK : (j + 1) * RANK] for j in range(chunks)], axis=1)
     packed = total[chunks * RANK :]
     gram = jnp.concatenate([packed[:, RANK * k : RANK * (k + 1)] for k in range(4)], axis=0)
     low = inverse_factor(gram)
-    f = jnp.dot(low, t, precision=lax.Precision.HIGHEST, preferred_element_type=F32)
-    z = lax.dot_general(low, f, (((0,), (0,)), ((), ())), precision=lax.Precision.HIGHEST, preferred_element_type=F32)
+    t = jnp.concatenate([total[j * RANK : (j + 1) * RANK] for j in range(chunks)], axis=1)
+    inner = (((0,), (0,)), ((), ()))
+    solve = lax.dot_general(left_terms(low, 0), right_terms(low), inner, preferred_element_type=F32)
+    z = jnp.dot(left_terms(solve, 1), right_terms(t), preferred_element_type=F32)
     z1, z2, _ = split3(z)
     right = jnp.concatenate([z1, z2, z1], axis=0)
+    copies = []
     for k in range(parts):
         p1, p2, _ = split3(p_ref[k])
         left = jnp.concatenate([p1, p1, p2], axis=0)
-        rebuilt = lax.dot_general(left, right, (((0,), (0,)), ((), ())), preferred_element_type=F32)
+        rebuilt = lax.dot_general(left, right, inner, preferred_element_type=F32)
         at = pl.ds(k * step, step)
-        comp_ref[at] = rebuilt.astype(BF16)
-        err_ref[at] = (c_ref[at].astype(F32) - rebuilt).astype(BF16)
+        comp[at] = rebuilt.astype(BF16)
+        copies.append(pltpu.make_async_copy(comp.at[at], comp_hbm.at[at], sems.at[2 * k]))
+        copies[-1].start()
+        err[at] = (c_ref[at].astype(F32) - rebuilt).astype(BF16)
+        copies.append(pltpu.make_async_copy(err.at[at], err_hbm.at[at], sems.at[2 * k + 1]))
+        copies[-1].start()
+    for copy in copies:
+        copy.wait()
 
 
 def last(x, p, c):
     return pl.pallas_call(
         last_kernel,
+        out_specs=[pl.BlockSpec(memory_space=pltpu.HBM)] * 2,
         out_shape=[jax.ShapeDtypeStruct(c.shape, BF16)] * 2,
+        scratch_shapes=[VMEM(c.shape, BF16), VMEM(c.shape, BF16), pltpu.SemaphoreType.DMA((2 * p.shape[0],))],
         compiler_params=pltpu.CompilerParams(vmem_limit_bytes=24 << 20),
         name="last",
     )(x, p, c)
@@ -150,7 +183,7 @@
     return list(table.values())
 
 
-def shards(near, far, y_groups, x_groups, gradients, errors, start_factor):
+def shards(near, far, plane, gradients, errors, start_factor):
     def exchange(x, axis, members):
         return lax.all_to_all(x, axis, 0, 0, tiled=True, axis_index_groups=members)
 
@@ -161,12 +194,22 @@
     piece = exchange(piece, "dp", far)
     piece = sum_copies(piece, parts)
     p = exchange(piece, "dp", near)
-    t = product(p, c, len(y_groups[0]))
-    t = exchange(t, "fsdp", y_groups)
-    t = sum_copies(t, len(x_groups[0]))
-    t = exchange(t, "fsdp", x_groups)
+    t = product(p, c, len(plane[0][0]))
+    t = exchange(t, ("dp", "fsdp"), plane[0])
+    t = sum_copies(t, len(plane[1][0]))
+    t = exchange(t, ("dp", "fsdp"), plane[1])
     compressed, new_errors = last(t, p, c)
     return compressed[None], new_errors[None]
+
+
+def plane_groups(dp, fsdp, width, turn):
+    def key(i):
+        outer, inner = divmod(i, fsdp)
+        if outer % 2 == turn:
+            return outer, 0, inner // width
+        return outer, 1, inner % width
+
+    return groups(dp * fsdp, key)
 
 
 def solution(mesh):
@@ -175,8 +218,7 @@
         shards,
         groups(dp, lambda i: i // 4),
         groups(dp, lambda i: i % 4),
-        groups(fsdp, lambda i: i // 4),
-        groups(fsdp, lambda i: i % 4),
+        [plane_groups(dp, fsdp, 4, turn) for turn in range(2)],
     )
     return jax.shard_map(
         body,

time: 77.5 us -> 72.3 us (0.933)
  local copies, waits for them, and re-layouts: 3.25 us -> 0 us
  blocking collectives: 67 us -> 66 us
  Pallas kernels: 6.2 us -> 5.33 us
    unnamed x6 -> x0, local copies, waits for them, and re-layouts: 3.25 us -> none
    all_to_all x5, blocking collectives: 67 us -> 66 us  [exchange(): return lax.all_to_all(x, axis, 0, 0, tiled=True, axis_index_groups=members)]
    pallas_call x2, Pallas kernels: 5.69 us -> 4.82 us  [the longest x1 2.72 us: last(): pl.pallas_call(last_kernel, out_specs=[pl.BlockSpec(memory_space=pltpu.HB...]
where the time goes in v2:
time: 72.3 us; the launch traced here: 72 us
  blocking collectives  66 us (91%)
  Pallas kernels  5.33 us (7%)
    all_to_all x5, blocking collectives, exchange(): return lax.all_to_all(x, axis, 0, 0, tiled=True, axis_index_groups=members)  66 us
    pallas_call x1, Pallas kernels, last(): pl.pallas_call(last_kernel, out_specs=[pl.BlockSpec(memory_space=pltpu.HB...  2.72 us
    pallas_call x1, Pallas kernels, first(): pl.pallas_call(first_kernel, in_specs=[pl.BlockSpec(memory_space=pltpu.HB...  2.1 us

profile of v2, /device:TPU:2, one launch (start us, length us, event | category | flops | bytes accessed | tf_op | source)
XLA Modules:
  0.0 72.0 jit_solution(16829904676656578080)
XLA Ops:
  0.6 2.1 %first.1 = (bf16[512,896]{1,0:T(8,128)(2,1)S(1)}, f32[4,32,128]{2,1,0:T(8,128)S(1)}) custom-call(bf16[512,896]{1,0:T(8,128)(2,1)} %bitcast.5, bf16[512,896]{1,0:T(8,128)(2,1)} %bitcast.6, f32[32,896]{1,0:T(8,128)} %bitcast.7), custom_call_target="tpu_custom_call" | custom-call | tf_op jit(solution)/shard_map/first/pallas_call | solution.py:47
  2.7 7.1 %all_to_all.25.x_ref = f32[4,32,128]{2,1,0:T(8,128)S(1)} all-to-all(f32[4,32,128]{2,1,0:T(8,128)S(1)} %get-tuple-element.6), channel_id=1, replica_groups={{0,16,32,48},{64,80,96,112},{128,144,160,176},{192,208,224,240},{256,27..., dimensions={0} | all-to-all | bytes 131072 | tf_op jit(solution)/shard_map/all_to_all | solution.py:188
  9.9 29.4 %all_to_all.26.x_ref = f32[8,32,128]{2,1,0:T(8,128)S(1)} all-to-all(f32[8,32,128]{2,1,0:T(8,128)S(1)} %sum_copies.3), channel_id=1, replica_groups={{0,64,128,192,256,320,384,448},{16,80,144,208,272,336,400,464},{32,96,1..., dimensions={0} | all-to-all | bytes 262144 | tf_op jit(solution)/shard_map/all_to_all | solution.py:188
  39.2 6.5 %all_to_all.27.p_ref = f32[4,32,128]{2,1,0:T(8,128)S(1)} all-to-all(f32[4,32,128]{2,1,0:T(8,128)S(1)} %sum_copies.4), channel_id=1, replica_groups={{0,16,32,48},{64,80,96,112},{128,144,160,176},{192,208,224,240},{256,27..., dimensions={0} | all-to-all | bytes 131072 | tf_op jit(solution)/shard_map/all_to_all | solution.py:188
  45.7 0.5 product.1
  46.2 12.1 %all_to_all.28.x_ref = f32[4,232,128]{2,1,0:T(8,128)S(1)} all-to-all(f32[4,232,128]{2,1,0:T(8,128)S(1)} %product.1), channel_id=1, replica_groups={{0,1,2,3},{4,5,6,7},{8,9,10,11},{12,13,14,15},{16,20,24,28},{17,21,25,2..., dimensions={0} | all-to-all | bytes 950272 | tf_op jit(solution)/shard_map/all_to_all | solution.py:188
  58.3 11.0 %all_to_all.29.x_ref = f32[4,232,128]{2,1,0:T(8,128)S(1)} all-to-all(f32[4,232,128]{2,1,0:T(8,128)S(1)} %sum_copies.5), channel_id=1, replica_groups={{0,4,8,12},{1,5,9,13},{2,6,10,14},{3,7,11,15},{16,17,18,19},{20,21,22,2..., dimensions={0} | all-to-all | bytes 950272 | tf_op jit(solution)/shard_map/all_to_all | solution.py:188
  69.3 2.7 %last.1 = (bf16[512,896]{1,0:T(8,128)(2,1)}, bf16[512,896]{1,0:T(8,128)(2,1)}) custom-call(f32[4,232,128]{2,1,0:T(8,128)S(1)} %all_to_all.29.x_ref, f32[4,32,128]{2,1,0:T(8,128)S(1)} %all_to_all.27.p_ref, bf16[512,896]{1,0:T(8,128)(2,1)S(1)} %get-tuple-element.7.c_ref), custom_call_target="tpu_custom_call" | custom-call | tf_op jit(solution)/shard_map/last/pallas_call | solution.py:169
  (3 shorter events, 0.1 us)

commit v3 on v2

v3 whole, which is shorter than its diff:
```python
import functools

import jax
import jax.numpy as jnp
from jax import lax
from jax.experimental import pallas as pl
from jax.experimental.pallas import tpu as pltpu
from jax.sharding import PartitionSpec as P

F32 = jnp.float32
LINE = [10, 11, 12, 13, 14, 15, 0, 1, 2, 3, 4, 5, 6, 7, 8, 9]
NEAR = [3, 2, 5, 1, 4, 7, 0, 6]
PLANE = [[2, 0, 1, 3], [2, 0, 1, 3]]
BF16 = jnp.bfloat16
RANK = 32
VMEM = pltpu.VMEM


def split3(x):
    a = x.astype(BF16)
    r = x - a.astype(F32)
    b = r.astype(BF16)
    c = (r - b.astype(F32)).astype(BF16)
    return a, b, c


def core_index():
    return lax.rem(lax.axis_index("dp"), 2)


def half_kernel(own, g_hbm, e_hbm, s_hbm, c_ref, part_ref, g, e, s, sems):
    parts, _, step = part_ref.shape
    half = core_index() if own else 1 - core_index()
    base = half * (parts * step)
    copies = [pltpu.make_async_copy(s_hbm, s, sems.at[0])]
    for k in range(parts):
        at, to = pl.ds(pl.multiple_of(base + k * step, step), step), pl.ds(k * step, step)
        copies.append(pltpu.make_async_copy(g_hbm.at[at], g.at[to], sems.at[2 * k + 1]))
        copies.append(pltpu.make_async_copy(e_hbm.at[at], e.at[to], sems.at[2 * k + 2]))
    for copy in copies:
        copy.start()
    copies[0].wait()
    q = s[...].astype(BF16)
    for k in range(parts):
        copies[2 * k + 1].wait()
        copies[2 * k + 2].wait()
        at = pl.ds(k * step, step)
        c = (g[at].astype(F32) + e[at].astype(F32)).astype(BF16)
        c_ref[at] = c
        part_ref[k] = lax.dot_general(q, c, (((1,), (1,)), ((), ())), preferred_element_type=F32)


def half_product(g, e, s, parts, own):
    rows, cols = g.shape
    rows //= 2
    step = rows // parts
    return pl.pallas_call(
        functools.partial(half_kernel, own),
        in_specs=[pl.BlockSpec(memory_space=pltpu.HBM)] * 3,
        out_shape=[
            jax.ShapeDtypeStruct((rows, cols), BF16),
            jax.ShapeDtypeStruct((parts, RANK, step), F32),
        ],
        scratch_shapes=[
            VMEM((rows, cols), BF16),
            VMEM((rows, cols), BF16),
            VMEM((RANK, cols), F32),
            pltpu.SemaphoreType.DMA((2 * parts + 1,)),
        ],
        compiler_params=pltpu.CompilerParams(vmem_limit_bytes=16 << 20),
        cost_estimate=pl.CostEstimate(flops=2 * RANK * rows * cols, bytes_accessed=6 * rows * cols, transcendentals=0),
        name="own_half" if own else "other_half",
    )(*[pltpu.with_memory_space_constraint(x, pltpu.HBM) for x in (g, e, s)])


def add_kernel(order, x_ref, y_ref, o_ref):
    for k in sorted(set(order)):
        total = x_ref[k] + y_ref[k]
        for j, piece in enumerate(order):
            if piece == k:
                o_ref[j] = total


def add_copies(x, y, order):
    return pl.pallas_call(
        functools.partial(add_kernel, order),
        out_shape=jax.ShapeDtypeStruct((len(order),) + x.shape[1:], F32),
        compiler_params=pltpu.CompilerParams(vmem_limit_bytes=16 << 20),
        name="add_copies",
    )(x, y)


def sum_kernel(copies, x_ref, o_ref):
    total = x_ref[0]
    for k in range(1, x_ref.shape[0]):
        total = total + x_ref[k]
    for k in range(copies):
        o_ref[k] = total


def sum_copies(x, copies):
    return pl.pallas_call(
        functools.partial(sum_kernel, copies),
        out_shape=jax.ShapeDtypeStruct((copies,) + x.shape[1:], F32),
        compiler_params=pltpu.CompilerParams(vmem_limit_bytes=16 << 20),
        name="sum_copies",
    )(x)


def take(p_ref, index, half):
    at = [NEAR.index(2 * index + core) for core in range(2)]
    return p_ref[at[0] + half * (at[1] - at[0])]


def row_blocks(p_ref, blocks):
    depth = p_ref.shape[0] // 2
    per = depth // blocks
    found = []
    for half in (core_index(), 1 - core_index()):
        for k in range(blocks):
            found.append(jnp.concatenate([take(p_ref, per * k + j, half) for j in range(per)], axis=0))
    return found


def product_kernel(copies, p_ref, own_ref, other_ref, o_ref):
    rows = own_ref.shape[0]
    terms = [split3(b) for b in row_blocks(p_ref, rows // 128)]
    left = jnp.concatenate([jnp.concatenate([t[j] for t in terms], axis=1) for j in range(3)], axis=0)
    t3 = jnp.dot(left[:, :rows], own_ref[...], preferred_element_type=F32)
    t3 = t3 + jnp.dot(left[:, rows:], other_ref[...], preferred_element_type=F32)
    t = t3[:RANK] + t3[RANK : 2 * RANK] + t3[2 * RANK :]
    g3 = lax.dot_general(left, left, (((1,), (1,)), ((), ())), preferred_element_type=F32)
    gr = g3[:RANK] + g3[RANK : 2 * RANK] + g3[2 * RANK :]
    gram = gr[:, :RANK] + gr[:, RANK : 2 * RANK] + gr[:, 2 * RANK : 3 * RANK]
    packed = jnp.concatenate([gram[8 * k : 8 * k + 8] for k in range(4)], axis=1)
    chunks = own_ref.shape[1] // 128
    for k in range(copies):
        for j in range(chunks):
            o_ref[k, j * RANK : (j + 1) * RANK] = t[:, j * 128 : (j + 1) * 128]
        o_ref[k, chunks * RANK : chunks * RANK + 8] = packed


def product(p, own, other, copies):
    return pl.pallas_call(
        functools.partial(product_kernel, copies),
        out_shape=jax.ShapeDtypeStruct((copies, own.shape[1] // 128 * RANK + 8, 128), F32),
        compiler_params=pltpu.CompilerParams(vmem_limit_bytes=16 << 20),
        name="product",
    )(p, own, other)


def inverse_factor(gram, block=16):
    rows = lax.broadcasted_iota(jnp.int32, (RANK, 128), 0)
    cols = lax.broadcasted_iota(jnp.int32, (RANK, 128), 1)
    w = jnp.concatenate([gram, jnp.zeros((RANK, 128 - RANK), F32)], axis=1) + (rows + RANK == cols).astype(F32)
    pivot = jnp.ones((RANK, 128), F32)
    for first_col in range(0, RANK, block):
        wide = [jnp.broadcast_to(w[:, k : k + 1], (RANK, 128)) for k in range(first_col, first_col + block)]
        for j in range(block):
            k = first_col + j
            inv = 1.0 / wide[j][k : k + 1]
            pivot = jnp.where(rows == k, wide[j], pivot)
            col = jnp.where(rows > k, wide[j], 0.0) * inv
            for m in range(j + 1, block):
                wide[m] = wide[m] - col * wide[m][k : k + 1]
            w = w - col * w[k : k + 1]
    return (w / jnp.sqrt(pivot))[:, RANK : 2 * RANK]


def left_terms(x, axis):
    a, b, c = split3(x)
    return jnp.concatenate([a, a, b, a, b, c], axis=axis)


def right_terms(x):
    a, b, c = split3(x)
    return jnp.concatenate([a, b, a, c, b, a], axis=0)


def last_kernel(x_ref, p_ref, own_ref, other_ref, comp_hbm, err_hbm, comp, err, sems):
    rows, cols = own_ref.shape
    chunks = cols // 128
    step = 128
    total = x_ref[0]
    for k in range(1, x_ref.shape[0]):
        total = total + x_ref[k]
    packed = total[chunks * RANK :]
    gram = jnp.concatenate([packed[:, RANK * k : RANK * (k + 1)] for k in range(4)], axis=0)
    low = inverse_factor(gram)
    t = jnp.concatenate([total[j * RANK : (j + 1) * RANK] for j in range(chunks)], axis=1)
    inner = (((0,), (0,)), ((), ()))
    solve = lax.dot_general(left_terms(low, 0), right_terms(low), inner, preferred_element_type=F32)
    z = jnp.dot(left_terms(solve, 1), right_terms(t), preferred_element_type=F32)
    z1, z2, _ = split3(z)
    right = jnp.concatenate([z1, z2, z1], axis=0)
    copies = []
    for k, block in enumerate(row_blocks(p_ref, rows // step)):
        p1, p2, _ = split3(block)
        left = jnp.concatenate([p1, p1, p2], axis=0)
        rebuilt = lax.dot_general(left, right, inner, preferred_element_type=F32)
        own = k < rows // step
        c_ref = own_ref if own else other_ref
        half = core_index() if own else 1 - core_index()
        inside = (k * step) % rows
        at = pl.ds(k * step, step)
        to = pl.ds(pl.multiple_of(half * rows + inside, step), step)
        comp[at] = rebuilt.astype(BF16)
        copies.append(pltpu.make_async_copy(comp.at[at], comp_hbm.at[to], sems.at[2 * k]))
        copies[-1].start()
        err[at] = (c_ref[pl.ds(inside, step)].astype(F32) - rebuilt).astype(BF16)
        copies.append(pltpu.make_async_copy(err.at[at], err_hbm.at[to], sems.at[2 * k + 1]))
        copies[-1].start()
    for copy in copies:
        copy.wait()


def last(x, p, own, other):
    rows, cols = own.shape
    whole = (2 * rows, cols)
    return pl.pallas_call(
        last_kernel,
        out_specs=[pl.BlockSpec(memory_space=pltpu.HBM)] * 2,
        out_shape=[jax.ShapeDtypeStruct(whole, BF16)] * 2,
        scratch_shapes=[VMEM(whole, BF16), VMEM(whole, BF16), pltpu.SemaphoreType.DMA((4 * rows // 128,))],
        compiler_params=pltpu.CompilerParams(vmem_limit_bytes=24 << 20),
        name="last",
    )(x, p, own, other)


def groups(size, key):
    table = {}
    for i in range(size):
        table.setdefault(key(i), []).append(i)
    return list(table.values())


def shards(swap, line, near, plane, gradients, errors, start_factor):
    def exchange(x, axis, members):
        return lax.all_to_all(x, axis, 0, 0, tiled=True, axis_index_groups=members)

    g, e, s = gradients[0], errors[0], start_factor[0]
    other, theirs = half_product(g, e, s, 2, False)
    theirs = lax.ppermute(theirs, "dp", swap)
    own, mine = half_product(g, e, s, 2, True)
    depth = len(near[0]) // 2
    order = [member // 2 % depth for member in line[0]]
    piece = add_copies(mine.reshape(depth, -1, 128), theirs.reshape(depth, -1, 128), order)
    piece = exchange(piece, "dp", line)
    p = exchange(sum_copies(piece, len(near[0])), "dp", near)
    t = product(p, own, other, len(plane[0][0]))
    t = exchange(t, ("dp", "fsdp"), plane[0])
    t = sum_copies(t, len(plane[1][0]))
    t = exchange(t, ("dp", "fsdp"), plane[1])
    compressed, new_errors = last(t, p, own, other)
    return compressed[None], new_errors[None]


def plane_groups(dp, fsdp, width, turn):
    def key(i):
        outer, inner = divmod(i, fsdp)
        if outer % 2 == turn:
            return outer, 0, inner // width
        return outer, 1, inner % width

    return [[members[j] for j in PLANE[turn]] for members in groups(dp * fsdp, key)]


def solution(mesh):
    dp, fsdp = mesh.shape["dp"], mesh.shape["fsdp"]
    body = functools.partial(
        shards,
        [(i, i ^ 1) for i in range(dp)],
        [[2 * z + core for z in LINE] for core in range(2)],
        [[first + member for member in NEAR] for first in range(0, dp, len(NEAR))],
        [plane_groups(dp, fsdp, 4, turn) for turn in range(2)],
    )
    placed = (P(None, "fsdp", "dp"), P(None, "fsdp", "dp"), P(None, None, "dp"))
    return jax.shard_map(body, mesh=mesh, in_specs=placed, out_specs=placed[:2], check_vma=False)
```

time: 72.3 us -> 62.4 us (0.86)
  the two profiles are of different devices: /device:TPU:2 before, /device:TPU:20 now
where the time goes in v3:
time: 62.4 us; the launch traced here: 62 us
  blocking collectives  53.1 us (85%)
  Pallas kernels  6.31 us (10%)
  starting transfers between devices  1.92 us (3%)
  between operations  0.68 us (1%)
    all_to_all x4, blocking collectives, exchange(): return lax.all_to_all(x, axis, 0, 0, tiled=True, axis_index_groups=members)  53.1 us
    pallas_call x2, Pallas kernels, half_product(): pl.pallas_call(functools.partial(half_kernel, own), in_specs=[pl.BlockSpe...  3.21 us
    pallas_call x1, Pallas kernels, last(): pl.pallas_call(last_kernel, out_specs=[pl.BlockSpec(memory_space=pltpu.HB...  2.57 us
    ppermute x1, starting transfers between devices, shards(): theirs = lax.ppermute(theirs, 'dp', swap)  1.92 us
  transfers between devices with their start and end apart: 1, of which 0 were waited for; matrix products, arithmetic and copies ran while one was open for 0% of the time, Pallas kernels for 3%

profile of v3, /device:TPU:20, one launch (start us, length us, event | category | flops | bytes accessed | tf_op | source)
XLA Modules:
  0.0 62.0 jit_solution(3646269024708973341)
XLA Ops:
  0.6 1.6 %other_half.1 = (bf16[256,896]{1,0:T(8,128)(2,1)S(1)}, f32[2,32,128]{2,1,0:T(8,128)S(1)}) custom-call(bf16[512,896]{1,0:T(8,128)(2,1)} %bitcast.9, bf16[512,896]{1,0:T(8,128)(2,1)} %bitcast.11, f32[32,896]{1,0:T(8,128)} %bitcast.13), custom_call_target="tpu_custom_call" | custom-call | flops 14680064 | bytes 1376256 | tf_op jit(solution)/shard_map/other_half/pallas_call | solution.py:57
  2.2 1.9 %collective-permute-start = (f32[2,32,128]{2,1,0:T(8,128)S(1)}, f32[2,32,128]{2,1,0:T(8,128)S(1)}, u32[]{:S(2)}, u32[]{:S(2)}) collective-permute-start(f32[2,32,128]{2,1,0:T(8,128)S(1)} %get-tuple-element.9), channel_id=1, source_target_pairs={{0,16},{16,0},{32,48},{48,32},{64,80},{80,64},{96,112},{112,96},{1... | collective-permute-start | bytes 98312 | tf_op jit(solution)/shard_map/ppermute | solution.py:243
  4.2 1.6 %own_half.1 = (bf16[256,896]{1,0:T(8,128)(2,1)S(1)}, f32[2,32,128]{2,1,0:T(8,128)S(1)}) custom-call(bf16[512,896]{1,0:T(8,128)(2,1)} %bitcast.10, bf16[512,896]{1,0:T(8,128)(2,1)} %bitcast.12, f32[32,896]{1,0:T(8,128)} %bitcast.14), custom_call_target="tpu_custom_call" | custom-call | flops 14680064 | bytes 1376256 | tf_op jit(solution)/shard_map/own_half/pallas_call | solution.py:57
  5.8 0.0 collective-permute-done
  5.8 25.7 %all_to_all.20.x_ref = f32[16,16,128]{2,1,0:T(8,128)S(1)} all-to-all(f32[16,16,128]{2,1,0:T(8,128)S(1)} %add_copies.1), channel_id=1, replica_groups={{320,352,384,416,448,480,0,32,64,96,128,160,192,224,256,288},{336,368,4..., dimensions={0} | all-to-all | bytes 262144 | tf_op jit(solution)/shard_map/all_to_all | solution.py:239
  31.6 7.0 %all_to_all.21.p_ref = f32[8,16,128]{2,1,0:T(8,128)S(1)} all-to-all(f32[8,16,128]{2,1,0:T(8,128)S(1)} %sum_copies.2), channel_id=1, replica_groups={{48,32,80,16,64,112,0,96},{176,160,208,144,192,240,128,224},{304,288,33..., dimensions={0} | all-to-all | bytes 131072 | tf_op jit(solution)/shard_map/all_to_all | solution.py:239
  38.6 0.5 product.1
  39.0 10.2 %all_to_all.22.x_ref = f32[4,232,128]{2,1,0:T(8,128)S(1)} all-to-all(f32[4,232,128]{2,1,0:T(8,128)S(1)} %product.1), channel_id=1, replica_groups={{2,0,1,3},{6,4,5,7},{10,8,9,11},{14,12,13,15},{24,16,20,28},{25,17,21,2..., dimensions={0} | all-to-all | bytes 950272 | tf_op jit(solution)/shard_map/all_to_all | solution.py:239
  49.3 10.2 %all_to_all.23.x_ref = f32[4,232,128]{2,1,0:T(8,128)S(1)} all-to-all(f32[4,232,128]{2,1,0:T(8,128)S(1)} %sum_copies.3), channel_id=1, replica_groups={{8,0,4,12},{9,1,5,13},{10,2,6,14},{11,3,7,15},{18,16,17,19},{22,20,21,2..., dimensions={0} | all-to-all | bytes 950272 | tf_op jit(solution)/shard_map/all_to_all | solution.py:239
  59.5 2.6 %last.1 = (bf16[512,896]{1,0:T(8,128)(2,1)}, bf16[512,896]{1,0:T(8,128)(2,1)}) custom-call(f32[4,232,128]{2,1,0:T(8,128)S(1)} %all_to_all.23.x_ref, f32[8,16,128]{2,1,0:T(8,128)S(1)} %all_to_all.21.p_ref, bf16[256,896]{1,0:T(8,128)(2,1)S(1)} %get-tuple-element.10.own_ref, bf16[256,896]{1,0:T(8,128)(2,1)S(1)} %get-tuple-element.11.other_ref), custom_call_target="tpu_custom_call" | custom-call | tf_op jit(solution)/shard_map/last/pallas_call | solution.py:220
  (3 shorter events, 0.1 us)
Async XLA Ops:
  2.2 3.5 %collective-permute-start = (f32[2,32,128]{2,1,0:T(8,128)S(1)}, f32[2,32,128]{2,1,0:T(8,128)S(1)}, u32[]{:S(2)}, u32[]{:S(2)}) collective-permute-start(f32[2,32,128]{2,1,0:T(8,128)S(1)} %get-tuple-element.9), channel_id=1, source_target_pairs={{0,16},{16,0},{32,48},{48,32},{64,80},{80,64},{96,112},{112,96},{1... | collective-permute-start | bytes 98312 | tf_op jit(solution)/shard_map/ppermute | solution.py:243

commit v4 on v3

--- a/solution.py
+++ b/solution.py
@@ -8,7 +8,7 @@
 from jax.sharding import PartitionSpec as P
 
 F32 = jnp.float32
-LINE = [10, 11, 12, 13, 14, 15, 0, 1, 2, 3, 4, 5, 6, 7, 8, 9]
+LINE = [10, 0, 1, 2, 3, 4, 5, 6, 7, 8, 9, 11, 12, 13, 14, 15]
 NEAR = [3, 2, 5, 1, 4, 7, 0, 6]
 PLANE = [[2, 0, 1, 3], [2, 0, 1, 3]]
 BF16 = jnp.bfloat16
@@ -28,49 +28,73 @@
     return lax.rem(lax.axis_index("dp"), 2)
 
 
-def half_kernel(own, g_hbm, e_hbm, s_hbm, c_ref, part_ref, g, e, s, sems):
+def first_kernel(g_hbm, e_hbm, s_hbm, own_ref, other_ref, q_ref, part_ref, g, e, s, sems):
     parts, _, step = part_ref.shape
-    half = core_index() if own else 1 - core_index()
-    base = half * (parts * step)
+    rows = parts * step
     copies = [pltpu.make_async_copy(s_hbm, s, sems.at[0])]
-    for k in range(parts):
-        at, to = pl.ds(pl.multiple_of(base + k * step, step), step), pl.ds(k * step, step)
+    for k in range(2 * parts):
+        half = 1 - core_index() if k < parts else core_index()
+        at = pl.ds(pl.multiple_of(half * rows + k % parts * step, step), step)
+        to = pl.ds(k * step, step)
         copies.append(pltpu.make_async_copy(g_hbm.at[at], g.at[to], sems.at[2 * k + 1]))
         copies.append(pltpu.make_async_copy(e_hbm.at[at], e.at[to], sems.at[2 * k + 2]))
     for copy in copies:
         copy.start()
     copies[0].wait()
     q = s[...].astype(BF16)
-    for k in range(parts):
+    q_ref[...] = q
+    for k in range(2 * parts):
         copies[2 * k + 1].wait()
         copies[2 * k + 2].wait()
         at = pl.ds(k * step, step)
         c = (g[at].astype(F32) + e[at].astype(F32)).astype(BF16)
-        c_ref[at] = c
-        part_ref[k] = lax.dot_general(q, c, (((1,), (1,)), ((), ())), preferred_element_type=F32)
-
-
-def half_product(g, e, s, parts, own):
+        to = pl.ds(k % parts * step, step)
+        if k < parts:
+            other_ref[to] = c
+            part_ref[k] = lax.dot_general(q, c, (((1,), (1,)), ((), ())), preferred_element_type=F32)
+        else:
+            own_ref[to] = c
+
+
+def first(g, e, s, parts):
     rows, cols = g.shape
-    rows //= 2
-    step = rows // parts
-    return pl.pallas_call(
-        functools.partial(half_kernel, own),
+    step = rows // (2 * parts)
+    return pl.pallas_call(
+        first_kernel,
         in_specs=[pl.BlockSpec(memory_space=pltpu.HBM)] * 3,
         out_shape=[
-            jax.ShapeDtypeStruct((rows, cols), BF16),
+            jax.ShapeDtypeStruct((rows // 2, cols), BF16),
+            jax.ShapeDtypeStruct((rows // 2, cols), BF16),
+            jax.ShapeDtypeStruct((RANK, cols), BF16),
             jax.ShapeDtypeStruct((parts, RANK, step), F32),
         ],
         scratch_shapes=[
             VMEM((rows, cols), BF16),
             VMEM((rows, cols), BF16),
             VMEM((RANK, cols), F32),
-            pltpu.SemaphoreType.DMA((2 * parts + 1,)),
+            pltpu.SemaphoreType.DMA((4 * parts + 1,)),
         ],
         compiler_params=pltpu.CompilerParams(vmem_limit_bytes=16 << 20),
-        cost_estimate=pl.CostEstimate(flops=2 * RANK * rows * cols, bytes_accessed=6 * rows * cols, transcendentals=0),
-        name="own_half" if own else "other_half",
+        name="first",
     )(*[pltpu.with_memory_space_constraint(x, pltpu.HBM) for x in (g, e, s)])
+
+
+def own_kernel(q_ref, c_ref, part_ref):
+    parts, _, step = part_ref.shape
+    for k in range(parts):
+        c = c_ref[pl.ds(k * step, step)]
+        part_ref[k] = lax.dot_general(q_ref[...], c, (((1,), (1,)), ((), ())), preferred_element_type=F32)
+
+
+def own_product(q, c, parts):
+    rows, cols = c.shape
+    return pl.pallas_call(
+        own_kernel,
+        out_shape=jax.ShapeDtypeStruct((parts, RANK, rows // parts), F32),
+        compiler_params=pltpu.CompilerParams(vmem_limit_bytes=16 << 20),
+        cost_estimate=pl.CostEstimate(flops=2 * RANK * rows * cols, bytes_accessed=2 * rows * cols, transcendentals=0),
+        name="own_product",
+    )(q, c)
 
 
 def add_kernel(order, x_ref, y_ref, o_ref):
@@ -239,9 +263,9 @@
         return lax.all_to_all(x, axis, 0, 0, tiled=True, axis_index_groups=members)
 
     g, e, s = gradients[0], errors[0], start_factor[0]
-    other, theirs = half_product(g, e, s, 2, False)
+    own, other, q, theirs = first(g, e, s, 2)
     theirs = lax.ppermute(theirs, "dp", swap)
-    own, mine = half_product(g, e, s, 2, True)
+    mine = own_product(q, own, 2)
     depth = len(near[0]) // 2
     order = [member // 2 % depth for member in line[0]]
     piece = add_copies(mine.reshape(depth, -1, 128), theirs.reshape(depth, -1, 128), order)

time: 62.4 us -> 61.7 us (0.989)
  Pallas kernels: 6.31 us -> 5.09 us
  waiting for transfers between devices: 0.01 us -> 0.94 us
    pallas_call x2, Pallas kernels: 3.21 us -> 1.99 us  [the longest x1 1.76 us: first(): pl.pallas_call(first_kernel, in_specs=[pl.BlockSpec(memory_space=pltpu.HB...]
    ppermute x1, waiting for transfers between devices: 0.01 us -> 0.94 us  [shards(): theirs = lax.ppermute(theirs, 'dp', swap)]
  transfers between devices with their start and end apart: 1 -> 1, of which waited for: 0 -> 1; matrix products, arithmetic and copies ran while one was open for 0% -> 0% of each run, Pallas kernels for 3% -> 0%
where the time goes in v4:
time: 61.7 us; the launch traced here: 61.4 us
  blocking collectives  52.8 us (86%)
  Pallas kernels  5.09 us (8%)
  starting transfers between devices  1.92 us (3%)
  waiting for transfers between devices  0.94 us (2%)
  between operations  0.66 us (1%)
    all_to_all x4, blocking collectives, exchange(): return lax.all_to_all(x, axis, 0, 0, tiled=True, axis_index_groups=members)  52.8 us
    pallas_call x1, Pallas kernels, last(): pl.pallas_call(last_kernel, out_specs=[pl.BlockSpec(memory_space=pltpu.HB...  2.58 us
    ppermute x1, starting transfers between devices, shards(): theirs = lax.ppermute(theirs, 'dp', swap)  1.92 us
    pallas_call x1, Pallas kernels, first(): pl.pallas_call(first_kernel, in_specs=[pl.BlockSpec(memory_space=pltpu.HB...  1.76 us
  transfers between devices with their start and end apart: 1, of which 1 were waited for; matrix products, arithmetic and copies ran while one was open for 0% of the time, Pallas kernels for 0%

profile of v4, /device:TPU:20, one launch (start us, length us, event | category | flops | bytes accessed | tf_op | source)
XLA Modules:
  0.0 61.4 jit_solution(2431797283538868532)
XLA Ops:
  0.6 1.8 %first.1 = (bf16[256,896]{1,0:T(8,128)(2,1)S(1)}, bf16[256,896]{1,0:T(8,128)(2,1)S(1)}, bf16[32,896]{1,0:T(8,128)(2,1)S(1)}, f32[2,32,128]{2,1,0:T(8,128)S(1)}) custom-call(bf16[512,896]{1,0:T(8,128)(2,1)} %bitcast.9, bf16[512,896]{1,0:T(8,128)(2,1)} %bitcast.10, f32[32,896]{1,0:T(8,128)} %bitcast.11), custom_call_target="tpu_custom_call" | custom-call | tf_op jit(solution)/shard_map/first/pallas_call | solution.py:62
  2.4 1.9 %collective-permute-start = (f32[2,32,128]{2,1,0:T(8,128)S(1)}, f32[2,32,128]{2,1,0:T(8,128)S(1)}, u32[]{:S(2)}, u32[]{:S(2)}) collective-permute-start(f32[2,32,128]{2,1,0:T(8,128)S(1)} %get-tuple-element.10), channel_id=1, source_target_pairs={{0,16},{16,0},{32,48},{48,32},{64,80},{80,64},{96,112},{112,96},{1... | collective-permute-start | bytes 98312 | tf_op jit(solution)/shard_map/ppermute | solution.py:267
  4.3 0.2 own_product.1
  4.6 0.9 %collective-permute-done = f32[2,32,128]{2,1,0:T(8,128)S(1)} collective-permute-done((f32[2,32,128]{2,1,0:T(8,128)S(1)}, f32[2,32,128]{2,1,0:T(8,128)S(1)}, u32[]{:S(2)}, u32[]{:S(2)}) %collective-permute-start) | collective-permute-done | bytes 32800 | tf_op jit(solution)/shard_map/ppermute | solution.py:267
  5.5 25.4 %all_to_all.20.x_ref = f32[16,16,128]{2,1,0:T(8,128)S(1)} all-to-all(f32[16,16,128]{2,1,0:T(8,128)S(1)} %add_copies.1), channel_id=1, replica_groups={{320,0,32,64,96,128,160,192,224,256,288,352,384,416,448,480},{336,16,48..., dimensions={0} | all-to-all | bytes 262144 | tf_op jit(solution)/shard_map/all_to_all | solution.py:263
  30.9 7.0 %all_to_all.21.p_ref = f32[8,16,128]{2,1,0:T(8,128)S(1)} all-to-all(f32[8,16,128]{2,1,0:T(8,128)S(1)} %sum_copies.2), channel_id=1, replica_groups={{48,32,80,16,64,112,0,96},{176,160,208,144,192,240,128,224},{304,288,33..., dimensions={0} | all-to-all | bytes 131072 | tf_op jit(solution)/shard_map/all_to_all | solution.py:263
  37.9 0.5 product.1
  38.4 10.2 %all_to_all.22.x_ref = f32[4,232,128]{2,1,0:T(8,128)S(1)} all-to-all(f32[4,232,128]{2,1,0:T(8,128)S(1)} %product.1), channel_id=1, replica_groups={{2,0,1,3},{6,4,5,7},{10,8,9,11},{14,12,13,15},{24,16,20,28},{25,17,21,2..., dimensions={0} | all-to-all | bytes 950272 | tf_op jit(solution)/shard_map/all_to_all | solution.py:263
  48.6 10.2 %all_to_all.23.x_ref = f32[4,232,128]{2,1,0:T(8,128)S(1)} all-to-all(f32[4,232,128]{2,1,0:T(8,128)S(1)} %sum_copies.3), channel_id=1, replica_groups={{8,0,4,12},{9,1,5,13},{10,2,6,14},{11,3,7,15},{18,16,17,19},{22,20,21,2..., dimensions={0} | all-to-all | bytes 950272 | tf_op jit(solution)/shard_map/all_to_all | solution.py:263
  58.8 2.6 %last.1 = (bf16[512,896]{1,0:T(8,128)(2,1)}, bf16[512,896]{1,0:T(8,128)(2,1)}) custom-call(f32[4,232,128]{2,1,0:T(8,128)S(1)} %all_to_all.23.x_ref, f32[8,16,128]{2,1,0:T(8,128)S(1)} %all_to_all.21.p_ref, bf16[256,896]{1,0:T(8,128)(2,1)S(1)} %get-tuple-element.9.c_ref.own_ref, bf16[256,896]{1,0:T(8,128)(2,1)S(1)} %get-tuple-element.11.other_ref), custom_call_target="tpu_custom_call" | custom-call | tf_op jit(solution)/shard_map/last/pallas_call | solution.py:244
  (3 shorter events, 0.1 us)
Async XLA Ops:
  2.4 3.1 %collective-permute-start = (f32[2,32,128]{2,1,0:T(8,128)S(1)}, f32[2,32,128]{2,1,0:T(8,128)S(1)}, u32[]{:S(2)}, u32[]{:S(2)}) collective-permute-start(f32[2,32,128]{2,1,0:T(8,128)S(1)} %get-tuple-element.10), channel_id=1, source_target_pairs={{0,16},{16,0},{32,48},{48,32},{64,80},{80,64},{96,112},{112,96},{1... | collective-permute-start | bytes 98312 | tf_op jit(solution)/shard_map/ppermute | solution.py:267

commit v5 on v4

--- a/solution.py
+++ b/solution.py
@@ -12,6 +12,7 @@
 NEAR = [3, 2, 5, 1, 4, 7, 0, 6]
 PLANE = [[2, 0, 1, 3], [2, 0, 1, 3]]
 BF16 = jnp.bfloat16
+LIFT = 2.0**60
 RANK = 32
 VMEM = pltpu.VMEM
 
@@ -150,8 +151,9 @@
     rows = own_ref.shape[0]
     terms = [split3(b) for b in row_blocks(p_ref, rows // 128)]
     left = jnp.concatenate([jnp.concatenate([t[j] for t in terms], axis=1) for j in range(3)], axis=0)
-    t3 = jnp.dot(left[:, :rows], own_ref[...], preferred_element_type=F32)
-    t3 = t3 + jnp.dot(left[:, rows:], other_ref[...], preferred_element_type=F32)
+    lifted = left * jnp.asarray(LIFT, BF16)
+    t3 = jnp.dot(lifted[:, :rows], own_ref[...], preferred_element_type=F32)
+    t3 = t3 + jnp.dot(lifted[:, rows:], other_ref[...], preferred_element_type=F32)
     t = t3[:RANK] + t3[RANK : 2 * RANK] + t3[2 * RANK :]
     g3 = lax.dot_general(left, left, (((1,), (1,)), ((), ())), preferred_element_type=F32)
     gr = g3[:RANK] + g3[RANK : 2 * RANK] + g3[2 * RANK :]
@@ -215,7 +217,7 @@
     inner = (((0,), (0,)), ((), ()))
     solve = lax.dot_general(left_terms(low, 0), right_terms(low), inner, preferred_element_type=F32)
     z = jnp.dot(left_terms(solve, 1), right_terms(t), preferred_element_type=F32)
-    z1, z2, _ = split3(z)
+    z1, z2, _ = split3(z * (1.0 / LIFT))
     right = jnp.concatenate([z1, z2, z1], axis=0)
     copies = []
     for k, block in enumerate(row_blocks(p_ref, rows // step)):

time: 61.7 us -> 61.7 us (level)
  no operation moved by 1% of the time
where the time goes in v5:
time: 61.7 us; the launch traced here: 61.4 us
  blocking collectives  52.8 us (86%)
  Pallas kernels  5.09 us (8%)
  starting transfers between devices  1.92 us (3%)
  waiting for transfers between devices  0.94 us (2%)
  between operations  0.66 us (1%)
    all_to_all x4, blocking collectives, exchange(): return lax.all_to_all(x, axis, 0, 0, tiled=True, axis_index_groups=members)  52.8 us
    pallas_call x1, Pallas kernels, last(): pl.pallas_call(last_kernel, out_specs=[pl.BlockSpec(memory_space=pltpu.HB...  2.58 us
    ppermute x1, starting transfers between devices, shards(): theirs = lax.ppermute(theirs, 'dp', swap)  1.92 us
    pallas_call x1, Pallas kernels, first(): pl.pallas_call(first_kernel, in_specs=[pl.BlockSpec(memory_space=pltpu.HB...  1.76 us
  transfers between devices with their start and end apart: 1, of which 1 were waited for; matrix products, arithmetic and copies ran while one was open for 0% of the time, Pallas kernels for 0%

profile of v5, /device:TPU:20, one launch (start us, length us, event | category | flops | bytes accessed | tf_op | source)
XLA Modules:
  0.0 61.4 jit_solution(1710366270934100152)
XLA Ops:
  0.6 1.8 %first.1 = (bf16[256,896]{1,0:T(8,128)(2,1)S(1)}, bf16[256,896]{1,0:T(8,128)(2,1)S(1)}, bf16[32,896]{1,0:T(8,128)(2,1)S(1)}, f32[2,32,128]{2,1,0:T(8,128)S(1)}) custom-call(bf16[512,896]{1,0:T(8,128)(2,1)} %bitcast.9, bf16[512,896]{1,0:T(8,128)(2,1)} %bitcast.10, f32[32,896]{1,0:T(8,128)} %bitcast.11), custom_call_target="tpu_custom_call" | custom-call | tf_op jit(solution)/shard_map/first/pallas_call | solution.py:63
  2.4 1.9 %collective-permute-start = (f32[2,32,128]{2,1,0:T(8,128)S(1)}, f32[2,32,128]{2,1,0:T(8,128)S(1)}, u32[]{:S(2)}, u32[]{:S(2)}) collective-permute-start(f32[2,32,128]{2,1,0:T(8,128)S(1)} %get-tuple-element.10), channel_id=1, source_target_pairs={{0,16},{16,0},{32,48},{48,32},{64,80},{80,64},{96,112},{112,96},{1... | collective-permute-start | bytes 98312 | tf_op jit(solution)/shard_map/ppermute | solution.py:269
  4.3 0.2 own_product.1
  4.6 0.9 %collective-permute-done = f32[2,32,128]{2,1,0:T(8,128)S(1)} collective-permute-done((f32[2,32,128]{2,1,0:T(8,128)S(1)}, f32[2,32,128]{2,1,0:T(8,128)S(1)}, u32[]{:S(2)}, u32[]{:S(2)}) %collective-permute-start) | collective-permute-done | bytes 32800 | tf_op jit(solution)/shard_map/ppermute | solution.py:269
  5.5 25.4 %all_to_all.20.x_ref = f32[16,16,128]{2,1,0:T(8,128)S(1)} all-to-all(f32[16,16,128]{2,1,0:T(8,128)S(1)} %add_copies.1), channel_id=1, replica_groups={{320,0,32,64,96,128,160,192,224,256,288,352,384,416,448,480},{336,16,48..., dimensions={0} | all-to-all | bytes 262144 | tf_op jit(solution)/shard_map/all_to_all | solution.py:265
  30.9 7.0 %all_to_all.21.p_ref = f32[8,16,128]{2,1,0:T(8,128)S(1)} all-to-all(f32[8,16,128]{2,1,0:T(8,128)S(1)} %sum_copies.2), channel_id=1, replica_groups={{48,32,80,16,64,112,0,96},{176,160,208,144,192,240,128,224},{304,288,33..., dimensions={0} | all-to-all | bytes 131072 | tf_op jit(solution)/shard_map/all_to_all | solution.py:265
  37.9 0.5 product.1
  38.4 10.2 %all_to_all.22.x_ref = f32[4,232,128]{2,1,0:T(8,128)S(1)} all-to-all(f32[4,232,128]{2,1,0:T(8,128)S(1)} %product.1), channel_id=1, replica_groups={{2,0,1,3},{6,4,5,7},{10,8,9,11},{14,12,13,15},{24,16,20,28},{25,17,21,2..., dimensions={0} | all-to-all | bytes 950272 | tf_op jit(solution)/shard_map/all_to_all | solution.py:265
  48.6 10.2 %all_to_all.23.x_ref = f32[4,232,128]{2,1,0:T(8,128)S(1)} all-to-all(f32[4,232,128]{2,1,0:T(8,128)S(1)} %sum_copies.3), channel_id=1, replica_groups={{8,0,4,12},{9,1,5,13},{10,2,6,14},{11,3,7,15},{18,16,17,19},{22,20,21,2..., dimensions={0} | all-to-all | bytes 950272 | tf_op jit(solution)/shard_map/all_to_all | solution.py:265
  58.8 2.6 %last.1 = (bf16[512,896]{1,0:T(8,128)(2,1)}, bf16[512,896]{1,0:T(8,128)(2,1)}) custom-call(f32[4,232,128]{2,1,0:T(8,128)S(1)} %all_to_all.23.x_ref, f32[8,16,128]{2,1,0:T(8,128)S(1)} %all_to_all.21.p_ref, bf16[256,896]{1,0:T(8,128)(2,1)S(1)} %get-tuple-element.9.c_ref.own_ref, bf16[256,896]{1,0:T(8,128)(2,1)S(1)} %get-tuple-element.11.other_ref), custom_call_target="tpu_custom_call" | custom-call | tf_op jit(solution)/shard_map/last/pallas_call | solution.py:246
  (3 shorter events, 0.1 us)
Async XLA Ops:
  2.4 3.1 %collective-permute-start = (f32[2,32,128]{2,1,0:T(8,128)S(1)}, f32[2,32,128]{2,1,0:T(8,128)S(1)}, u32[]{:S(2)}, u32[]{:S(2)}) collective-permute-start(f32[2,32,128]{2,1,0:T(8,128)S(1)} %get-tuple-element.10), channel_id=1, source_target_pairs={{0,16},{16,0},{32,48},{48,32},{64,80},{80,64},{96,112},{112,96},{1... | collective-permute-start | bytes 98312 | tf_op jit(solution)/shard_map/ppermute | solution.py:269
